TPU v7x, 32 devices: a whole 2x2x4 slice. The times are simulated.
32 devices in a mesh: dp: 8 (over z, core), ctx: 4 (over y, x).
Axes of the slice: x: 2, y: 2, z: 4, core: 2. Of those that a mesh axis runs over, the one named last changes fastest.
Arguments:
- loader_rows: bfloat16 [8192, 512], P(('dp', 'ctx')), may hold values from -60 to 60
- send_slot: int32 [8192], P(('dp', 'ctx')), may hold values from 0 to 383, as said below
- arrive_slot: int32 [8192], P(('dp', 'ctx')), may hold values from 0 to 383, as said below
- user_lengths: int32 [8, 4], P('dp'), may hold values from 1 to 768, 1024 in all within a row
- proj_weight: bfloat16 [512, 2048], replicated, may hold values from -0.25 to 0.25
- out_weight: bfloat16 [512, 512], replicated, may hold values from -0.25 to 0.25
- cotangent: bfloat16 [8192, 512], P(('dp', 'ctx')), may hold values from -6 to 6
Outputs:
- layer_out: bfloat16 [8192, 512], P(('dp', 'ctx'))
- row_grads: bfloat16 [8192, 512], P(('dp', 'ctx'))
- proj_grad: float32 [512, 2048], replicated
- out_grad: float32 [512, 512], replicated
Inputs may be any that keep to these rules, and one draw needn't show every extreme that they name: `send_slot`: on each loader device its 256 entries are distinct slots d * 12 + k, d the owner device and k counting that owner's rows from this loader from 0; no loader sends more than 12 rows to one owner and some pairs send exactly 12; the number of rows from loader s to owner d depends only on (d - s) mod (8 * 4). `arrive_slot`: on each owner device its 256 entries are distinct slots s * 12 + k, the k-th row that loader s sends to it; every owner receives exactly 256 rows.
All inputs are finite; a program needn't handle non-finite values.
Results may differ from a plain program's by a relative error of at most 0.009.
Values may be sent and summed in bfloat16 or wider, within the bound.
No kernel may reach another device: no remote copies, remote signals or barrier semaphores. Data moves between devices by JAX's collectives and lax.ppermute only.
A program may use at most 128 MiB of HBM per device.

v0:
```python
import jax
import jax.numpy as jnp
from jax import lax
from jax.sharding import PartitionSpec as P

HEADS = 8
norm_eps = 1e-05


def normalize(values):
    centre = values - jnp.mean(values, axis=-1, keepdims=True)
    inverse = lax.rsqrt(jnp.mean(centre * centre, axis=-1, keepdims=True) + norm_eps)
    return (centre * inverse, inverse)


def normalize_back(grad_in, normed, inverse):
    mean_grad = jnp.mean(grad_in, axis=-1, keepdims=True)
    mean_cross = jnp.mean(grad_in * normed, axis=-1, keepdims=True)
    return (grad_in - mean_grad - normed * mean_cross) * inverse


def silu_grad(values):
    sigma = jax.nn.sigmoid(values)
    return sigma * (1.0 + values * (1.0 - sigma))


def in_blocks(step_fn, block_rows, running, pieces):
    total_rows = pieces[0].shape[0]

    def one_block(index, carry):
        start = index * block_rows
        sliced = tuple((lax.dynamic_slice_in_dim(each, start, block_rows, 0) for each in pieces))
        return step_fn(carry, sliced, start)

    return lax.fori_loop(0, total_rows // block_rows, one_block, running)


def local(loader_rows, send_slot, arrive_slot, user_lengths, proj_weight, out_weight, cotangent):
    row_count = send_slot.shape[0]
    model_width = out_weight.shape[0]
    head_dim = model_width // HEADS
    score_scale = head_dim ** (-0.5)
    group_size = lax.axis_size("ctx")
    group_count = lax.axis_size("dp")
    device_count = group_size * group_count
    per_pair = row_count // device_count
    capacity = per_pair + max(1, per_pair // 2)
    half_rows = row_count // 2
    group_total = group_size * row_count
    outgoing = (
        jnp.zeros((device_count * capacity, model_width), jnp.bfloat16)
        .at[send_slot]
        .set(loader_rows)
    )
    arrived = lax.all_to_all(
        outgoing.reshape(device_count, capacity, model_width),
        ("dp", "ctx"),
        split_axis=0,
        concat_axis=0,
        tiled=True,
    )
    own_rows = arrived.reshape(device_count * capacity, model_width)[arrive_slot]
    ends = jnp.cumsum(user_lengths[0])

    def position_of(row_index):
        device_of = row_index // row_count
        local_of = row_index % row_count
        return jnp.where(
            local_of < half_rows,
            device_of * half_rows + local_of,
            group_total - (device_of + 1) * half_rows + (local_of - half_rows),
        )

    own_pos = position_of(
        lax.axis_index("ctx") * row_count + jnp.arange(row_count, dtype=jnp.int32)
    )

    def user_of(positions):
        return jnp.sum((ends[None, :] <= positions[:, None]).astype(jnp.int32), axis=1)

    own_users = user_of(own_pos)

    def allowed_of(query_pos, query_users, key_pos, key_users):
        return (key_pos[None, :] <= query_pos[:, None]) & (
            query_users[:, None] == key_users[None, :]
        )

    def split_heads(values):
        return values.reshape(values.shape[0], HEADS, head_dim)

    def merge_heads(values):
        return values.reshape(values.shape[0], model_width)

    def piece_scores(query_part, key_part):
        return (
            jnp.einsum(
                "qhd,khd->hqk",
                split_heads(query_part),
                split_heads(key_part),
                preferred_element_type=jnp.float32,
            )
            * score_scale
        )

    rows_f = own_rows.astype(jnp.float32)
    normed, inverse_in = normalize(rows_f)
    normed_bf = normed.astype(jnp.bfloat16)
    pre = jnp.dot(normed_bf, proj_weight, preferred_element_type=jnp.float32)
    proj = (pre * jax.nn.sigmoid(pre)).astype(jnp.bfloat16)
    update_rows = proj[:, :model_width]
    value_rows = proj[:, model_width : 2 * model_width]
    query_rows = proj[:, 2 * model_width : 3 * model_width]
    key_rows = proj[:, 3 * model_width :]

    def attend_block(running, pieces, first_row):
        key_part, value_part = pieces
        key_pos = position_of(first_row + jnp.arange(key_part.shape[0], dtype=jnp.int32))
        allowed = allowed_of(own_pos, own_users, key_pos, user_of(key_pos))[None]
        scores = piece_scores(query_rows, key_part)
        weights = jnp.where(allowed, scores * jax.nn.sigmoid(scores), 0.0).astype(jnp.bfloat16)
        product = jnp.einsum(
            "hqk,khd->qhd", weights, split_heads(value_part), preferred_element_type=jnp.float32
        )
        return running + merge_heads(product)

    zeros_rows = jnp.zeros((row_count, model_width), jnp.float32)
    attended = in_blocks(
        attend_block,
        row_count,
        zeros_rows,
        (
            lax.all_gather(key_rows, "ctx", axis=0, tiled=True),
            lax.all_gather(value_rows, "ctx", axis=0, tiled=True),
        ),
    )
    att_normed, inverse_att = normalize(attended)
    update_f = update_rows.astype(jnp.float32)
    gated = (att_normed * update_f).astype(jnp.bfloat16)
    layer_rows = (rows_f + jnp.dot(gated, out_weight, preferred_element_type=jnp.float32)).astype(
        jnp.bfloat16
    )
    out_term = jnp.dot(gated.T, cotangent, preferred_element_type=jnp.float32)
    grad_gated = jnp.dot(cotangent, out_weight.T, preferred_element_type=jnp.float32)
    grad_update = grad_gated * att_normed
    grad_att = normalize_back(grad_gated * update_f, att_normed, inverse_att).astype(jnp.bfloat16)

    def query_block(running, pieces, first_row):
        key_part, value_part = pieces
        key_pos = position_of(first_row + jnp.arange(key_part.shape[0], dtype=jnp.int32))
        allowed = allowed_of(own_pos, own_users, key_pos, user_of(key_pos))[None]
        scores = piece_scores(query_rows, key_part)
        grad_weights = jnp.einsum(
            "qhd,khd->hqk",
            split_heads(grad_att),
            split_heads(value_part),
            preferred_element_type=jnp.float32,
        )
        grad_scores = jnp.where(
            allowed, grad_weights * silu_grad(scores) * score_scale, 0.0
        ).astype(jnp.bfloat16)
        product = jnp.einsum(
            "hqk,khd->qhd", grad_scores, split_heads(key_part), preferred_element_type=jnp.float32
        )
        return running + merge_heads(product)

    def key_block(running, pieces, first_row):
        query_part, grad_part = pieces
        query_pos = position_of(first_row + jnp.arange(query_part.shape[0], dtype=jnp.int32))
        allowed = allowed_of(query_pos, user_of(query_pos), own_pos, own_users)[None]
        scores = piece_scores(query_part, key_rows)
        weights = jnp.where(allowed, scores * jax.nn.sigmoid(scores), 0.0).astype(jnp.bfloat16)
        grad_weights = jnp.einsum(
            "qhd,khd->hqk",
            split_heads(grad_part),
            split_heads(value_rows),
            preferred_element_type=jnp.float32,
        )
        grad_scores = jnp.where(
            allowed, grad_weights * silu_grad(scores) * score_scale, 0.0
        ).astype(jnp.bfloat16)
        grad_key = jnp.einsum(
            "hqk,qhd->khd", grad_scores, split_heads(query_part), preferred_element_type=jnp.float32
        )
        grad_value = jnp.einsum(
            "hqk,qhd->khd", weights, split_heads(grad_part), preferred_element_type=jnp.float32
        )
        return (running[0] + merge_heads(grad_key), running[1] + merge_heads(grad_value))

    grad_query = in_blocks(
        query_block,
        row_count,
        zeros_rows,
        (
            lax.all_gather(key_rows, "ctx", axis=0, tiled=True),
            lax.all_gather(value_rows, "ctx", axis=0, tiled=True),
        ),
    )
    grad_key, grad_value = in_blocks(
        key_block,
        row_count,
        (zeros_rows, zeros_rows),
        (
            lax.all_gather(query_rows, "ctx", axis=0, tiled=True),
            lax.all_gather(grad_att, "ctx", axis=0, tiled=True),
        ),
    )
    grad_proj = jnp.concatenate([grad_update, grad_value, grad_query, grad_key], axis=1)
    grad_pre = (grad_proj * silu_grad(pre)).astype(jnp.bfloat16)
    proj_term = jnp.dot(normed_bf.T, grad_pre, preferred_element_type=jnp.float32)
    grad_normed = jnp.dot(grad_pre, proj_weight.T, preferred_element_type=jnp.float32)
    row_grads = (
        cotangent.astype(jnp.float32) + normalize_back(grad_normed, normed, inverse_in)
    ).astype(jnp.bfloat16)
    proj_sum, out_sum = lax.psum((proj_term, out_term), ("dp", "ctx"))
    grad_scale = (row_count * device_count) ** (-0.5)
    return (layer_rows, row_grads, proj_sum * grad_scale, out_sum * grad_scale)


def solution(mesh):
    placed = (
        P(("dp", "ctx"), None),
        P(("dp", "ctx")),
        P(("dp", "ctx")),
        P("dp", None),
        P(),
        P(),
        P(("dp", "ctx"), None),
    )
    return jax.shard_map(
        local,
        mesh=mesh,
        in_specs=placed,
        out_specs=(P(("dp", "ctx"), None), P(("dp", "ctx"), None), P(), P()),
        check_vma=False,
    )
```

profile of v0, /device:TPU:0, one launch (start us, length us, event | category | flops | bytes accessed | tf_op | source)
XLA Modules:
  0.0 400.7 jit_solution(9366824799308477023)
XLA Ops:
  8.0 2.0 scatter_custom_fusion
  10.9 7.3 %all-to-all-start = ((bf16[32,12,512]{2,1,0:T(8,128)(2,1)}), bf16[32,12,512]{2,1,0:T(8,128)(2,1)S(1)}, u32[]{:S(2)}, u32[]{:S(2)}) async-start(bf16[32,12,512]{2,1,0:T(8,128)(2,1)} %reshape.616), calls=%async_computation | async-start | bytes 1048576 | tf_op jit(solution)/shard_map/all_to_all | solution.py:55
  18.4 16.2 %all-to-all-done = bf16[32,12,512]{2,1,0:T(8,128)(2,1)S(1)} async-done(((bf16[32,12,512]{2,1,0:T(8,128)(2,1)}), bf16[32,12,512]{2,1,0:T(8,128)(2,1)S(1)}, u32[]{:S(2)}, u32[]{:S(2)}) %all-to-all-start) | async-done | bytes 393248 | tf_op jit(solution)/shard_map/all_to_all | solution.py:55
  36.2 2.1 multiply_convert_fusion
  45.8 18.7 %all-gather.5.cloned.1.call-done = bf16[1024,512]{1,0:T(8,128)(2,1)} async-done(((bf16[256,512]{1,0:T(8,128)(2,1)}), bf16[1024,512]{1,0:T(8,128)(2,1)}) %all-gather.5.cloned.1.call-update) | async-done | bytes 1048592 | tf_op jit(solution)/shard_map/all_gather | solution.py:133
  64.5 2.3 copy.48
  66.8 26.7 %all-gather.7.cloned.1.call-done = bf16[1024,512]{1,0:T(8,128)(2,1)} async-done(((bf16[256,512]{1,0:T(8,128)(2,1)}), bf16[1024,512]{1,0:T(8,128)(2,1)}) %all-gather.7.cloned.1.call-update) | async-done | bytes 1048592 | tf_op jit(solution)/shard_map/all_gather | solution.py:132
  93.5 2.3 copy.49
  95.7 17.4 %while.50 = (s32[]{:T(128)}, f32[256,512]{0,1:T(8,128)S(1)}, bf16[1024,512]{0,1:T(8,128)(2,1)}, s32[256]{0:T(256)S(1)}, s32[4]{0:T(128)S(1)}, /*index=5*/bf16[10...) while((s32[]{:T(128)}, f32[256,512]{0,1:T(8,128)S(1)}, ...), condition=%wide.region_7.8_spmd.clone, body=%wide.region_5.7_spmd.clone.sunk | while | flops 138364160 | bytes 4071625 | solution.py:35
  97.9 2.1 fusion.118
  102.2 2.1 fusion.118
  106.6 2.1 fusion.118
  111.0 2.1 fusion.118
  115.4 2.1 multiply_convert_fusion.1
  118.6 46.4 %while.52 = (s32[]{:T(128)}, f32[256,512]{0,1:T(8,128)}, bf16[1024,512]{0,1:T(8,128)(2,1)}, s32[256]{0:T(256)S(1)}, s32[4]{0:T(128)S(1)}, /*index=5*/bf16[1024,5...) while((s32[]{:T(128)}, f32[256,512]{0,1:T(8,128)}, ...), condition=%wide.region_17.18_spmd.clone, body=%wide.region_15.17_spmd.clone.sunk | while | flops 208094464 | bytes 12984529 | solution.py:35
  119.9 3.2 fusion.133
  123.2 2.9 copy.73
  126.0 2.3 fusion.134
  130.7 3.2 fusion.133
  133.9 2.9 copy.73
  136.8 2.3 fusion.134
  142.7 3.2 fusion.133
  145.9 2.9 copy.73
  148.8 2.3 fusion.134
  154.5 3.2 fusion.133
  157.7 2.9 copy.73
  160.6 2.3 fusion.134
  164.9 2.1 copy.61
  167.0 2.3 fusion.70
  169.4 61.8 %while.51 = (s32[]{:T(128)}, f32[256,512]{0,1:T(8,128)S(1)}, f32[256,512]{0,1:T(8,128)}, bf16[1024,512]{1,0:T(8,128)(2,1)}, s32[4]{0:T(128)S(1)}, /*index=5*/s32...) while((s32[]{:T(128)}, f32[256,512]{0,1:T(8,128)S(1)}, ...), condition=%wide.region_14.15_spmd.clone, body=%wide.region_12.14_spmd.clone.sunk | while | flops 279135488 | bytes 18555156 | solution.py:35
  170.5 2.8 fusion.125
  175.4 3.8 fusion.127
  179.2 3.3 fusion.126
  185.9 2.8 fusion.125
  190.8 3.8 fusion.127
  194.6 3.3 fusion.126
  201.4 2.8 fusion.125
  206.2 3.8 fusion.127
  210.0 3.3 fusion.126
  216.8 2.8 fusion.125
  221.7 3.8 fusion.127
  225.5 3.3 fusion.126
  231.1 2.1 copy.60
  234.2 3.0 fusion.45
  237.2 2.9 fusion.63
  240.1 2.1 fusion.46
  244.1 144.0 %all-reduce.3.cloned.1.call-done = (f32[512,2048]{1,0:T(8,128)}, f32[512,512]{1,0:T(8,128)}) async-done(((f32[512,2048]{1,0:T(8,128)}, f32[512,512]{1,0:T(8,128)}), (f32[512,2048]{1,0:T(8,128)}, f32[512,512]{1,0:T(8,128)})) %all-reduce.3.cloned.1.call-update) | async-done | bytes 5242896 | tf_op jit(solution)/shard_map/psum | solution.py:214
  388.1 5.0 %broadcast_multiply_fusion = f32[512,2048]{1,0:T(8,128)} fusion(f32[512,2048]{1,0:T(8,128)} %get-tuple-element.919), kind=kLoop, calls=%fused_computation.106 | loop fusion | flops 1048576 | bytes 8388608 | tf_op jit(solution)/shard_map/mul | solution.py:216
  (157 shorter events, 61.4 us)
Async XLA Ops:
  7.2 29.0 %copy-start = (bf16[512,2048]{1,0:T(8,128)(2,1)S(1)}, bf16[512,2048]{1,0:T(8,128)(2,1)}, u32[]{:S(2)}) copy-start(bf16[512,2048]{1,0:T(8,128)(2,1)} %param.17) | copy-start | bytes 6291460
  7.2 11.1 %copy-start.9 = (s32[256]{0:T(256)S(1)}, s32[256]{0:T(256)}, u32[]{:S(2)}) copy-start(s32[256]{0:T(256)} %param.15) | copy-start | bytes 3076
  10.9 23.6 %all-to-all-start = ((bf16[32,12,512]{2,1,0:T(8,128)(2,1)}), bf16[32,12,512]{2,1,0:T(8,128)(2,1)S(1)}, u32[]{:S(2)}, u32[]{:S(2)}) async-start(bf16[32,12,512]{2,1,0:T(8,128)(2,1)} %reshape.616), calls=%async_computation | async-start | bytes 1048576 | tf_op jit(solution)/shard_map/all_to_all | solution.py:55
  18.3 46.2 %all-gather.5.cloned.1.call-start = ((), (), s32[]{:S(2)}) async-start(), calls=%async_computation.1 | async-start | bytes 1310720 | tf_op jit(solution)/shard_map/all_gather | solution.py:133
  38.3 1.0 copy-start.7
  38.3 2.7 copy-start.10
  40.1 5.6 %copy-start.5 = (bf16[256,512]{1,0:T(8,128)(2,1)}, bf16[256,512]{1,0:T(8,128)(2,1)S(1)}, u32[]{:S(2)}) copy-start(bf16[256,512]{1,0:T(8,128)(2,1)S(1)} %get-tuple-element.934) | copy-start | bytes 786436
  40.2 53.3 %all-gather.7.cloned.1.call-start = ((), (), s32[]{:S(2)}) async-start(), calls=%async_computation.2 | async-start | bytes 1310720 | tf_op jit(solution)/shard_map/all_gather | solution.py:132
  40.9 128.5 %all-gather.9.cloned.1.call-start = ((), (), s32[]{:S(2)}) async-start(), calls=%async_computation.3 | async-start | bytes 1310720 | tf_op jit(solution)/shard_map/all_gather | solution.py:203
  45.8 123.6 %all-gather.11.cloned.1.call-start = ((), (), s32[]{:S(2)}) async-start(), calls=%async_computation.4 | async-start | bytes 1310720 | tf_op jit(solution)/shard_map/all_gather | solution.py:204
  117.5 0.8 copy-start.4
  118.3 269.8 %all-reduce.3.cloned.1.call-start = ((), (), s32[]{:S(2)}) async-start(), calls=%async_computation.5 | async-start | bytes 10485760 | tf_op jit(solution)/shard_map/psum | solution.py:214
  164.9 4.4 %copy-start.1 = (f32[256,512]{0,1:T(8,128)S(1)}, f32[256,512]{0,1:T(8,128)}, u32[]{:S(2)}) copy-start(f32[256,512]{0,1:T(8,128)} %custom-call.1) | copy-start | bytes 1572868
  179.2 3.3 copy-start.2
  184.0 0.8 copy-start.3
  194.6 3.3 copy-start.2
  199.4 0.8 copy-start.3
  210.0 3.3 copy-start.2
  214.9 0.8 copy-start.3
  225.5 3.3 copy-start.2
  230.3 0.8 copy-start.3
  242.2 0.9 copy-start.6
  388.1 5.0 %copy-start.8 = (f32[512,512]{1,0:T(8,128)S(1)}, f32[512,512]{1,0:T(8,128)}, u32[]{:S(2)}) copy-start(f32[512,512]{1,0:T(8,128)} %get-tuple-element.920) | copy-start | bytes 3145732
Sparse Core Ops, SparseCore 0:
  40.3 24.1 all-gather.4
  66.9 26.4 all-gather.6
  95.3 26.5 all-gather.8
  123.6 26.4 all-gather.10
  240.2 147.8 all-reduce.2
where the time goes:
time: 403 us; the launch traced here: 401 us
  waiting for transfers between devices  206 us (51%)
  matrix products  82.1 us (20%)
  local copies, waits for them, and re-layouts  59.7 us (15%)
  other arithmetic  30.5 us (8%)
  between operations  14 us (3%)
  starting transfers between devices  7.71 us (2%)
    psum x1, waiting for transfers between devices, local(): proj_sum, out_sum = lax.psum((proj_term, out_term), ('dp', 'ctx'))  144 us
    all_gather x1, waiting for transfers between devices, local(): lax.all_gather(key_rows, 'ctx', axis=0, tiled=True)  26.7 us
    dot_general x8, matrix products, piece_scores(): jnp.einsum('qhd,khd->hqk', split_heads(query_part), split_heads(key_part)...  24.1 us
    dynamic_slice x24, local copies, waits for them, and re-layouts, one_block(): lax.dynamic_slice_in_dim(each, start, block_rows, 0)  23.5 us
    all_gather x1, waiting for transfers between devices, local(): lax.all_gather(value_rows, 'ctx', axis=0, tiled=True)  18.7 us
    all_to_all x1, waiting for transfers between devices, local(): lax.all_to_all(outgoing.reshape(device_count, capacity, model_width), ('d...  16.2 us
    dot_general x4, matrix products, key_block(): jnp.einsum('hqk,qhd->khd', grad_scores, split_heads(query_part), preferre...  15.2 us
    dot_general x4, matrix products, key_block(): jnp.einsum('hqk,qhd->khd', weights, split_heads(grad_part), preferred_ele...  13.1 us
  transfers between devices with their start and end apart: 6, of which 4 were waited for; matrix products, arithmetic and copies ran while one was open for 22% of the time, Pallas kernels for 0%

commit v1 on v0

--- a/solution.py
+++ b/solution.py
@@ -5,6 +5,18 @@
 
 HEADS = 8
 norm_eps = 1e-05
+
+
+def collect(x, axis, dim):
+    ways, here = (lax.axis_size(axis), lax.axis_index(axis))
+    grown, reach = (x, 1)
+    while reach < ways:
+        theirs = lax.ppermute(grown, axis, [(d, d ^ reach) for d in range(ways)])
+        mine_first = jnp.concatenate([grown, theirs], axis=dim)
+        theirs_first = jnp.concatenate([theirs, grown], axis=dim)
+        grown = jnp.where(here & reach == 0, mine_first, theirs_first)
+        reach = 2 * reach
+    return grown
 
 
 def normalize(values):
@@ -128,10 +140,7 @@
         attend_block,
         row_count,
         zeros_rows,
-        (
-            lax.all_gather(key_rows, "ctx", axis=0, tiled=True),
-            lax.all_gather(value_rows, "ctx", axis=0, tiled=True),
-        ),
+        (collect(key_rows, "ctx", 0), lax.all_gather(value_rows, "ctx", axis=0, tiled=True)),
     )
     att_normed, inverse_att = normalize(attended)
     update_f = update_rows.astype(jnp.float32)

time: 403 us -> 391 us (0.970)
  waiting for transfers between devices: 206 us -> 180 us
  local copies, waits for them, and re-layouts: 59.7 us -> 66.8 us
  other arithmetic: 30.5 us -> 35.4 us
    all_gather x1, waiting for transfers between devices: 26.7 us -> 0.02 us  [local(): lax.all_gather(key_rows, 'ctx', axis=0, tiled=True)]
    ppermute x0 -> x2, waiting for transfers between devices: none -> 21.2 us  [collect(): theirs = lax.ppermute(grown, axis, [(d, d ^ reach) for d in range(ways)])]
    all_gather x1, waiting for transfers between devices: 18.7 us -> 0.01 us  [local(): lax.all_gather(value_rows, 'ctx', axis=0, tiled=True)]
    dynamic_slice x24 -> x40, local copies, waits for them, and re-layouts: 23.5 us -> 34 us  [one_block(): lax.dynamic_slice_in_dim(each, start, block_rows, 0)]
    select_n x0 -> x2, other arithmetic: none -> 4.89 us  [collect(): grown = jnp.where(here & reach == 0, mine_first, theirs_first)]
    unnamed x24 -> x25, local copies, waits for them, and re-layouts: 10.9 us -> 7.71 us
  transfers between devices with their start and end apart: 6 -> 8, of which waited for: 4 -> 4; matrix products, arithmetic and copies ran while one was open for 22% -> 25% of each run, Pallas kernels for 0% -> 0%
where the time goes in v1:
time: 391 us; the launch traced here: 388 us
  waiting for transfers between devices  180 us (46%)
  matrix products  82 us (21%)
  local copies, waits for them, and re-layouts  66.8 us (17%)
  other arithmetic  35.4 us (9%)
  between operations  14 us (4%)
  starting transfers between devices  9.75 us (2%)
    psum x1, waiting for transfers between devices, local(): proj_sum, out_sum = lax.psum((proj_term, out_term), ('dp', 'ctx'))  142 us
    dynamic_slice x40, local copies, waits for them, and re-layouts, one_block(): lax.dynamic_slice_in_dim(each, start, block_rows, 0)  34 us
    dot_general x8, matrix products, piece_scores(): jnp.einsum('qhd,khd->hqk', split_heads(query_part), split_heads(key_part)...  24.1 us
    ppermute x2, waiting for transfers between devices, collect(): theirs = lax.ppermute(grown, axis, [(d, d ^ reach) for d in range(ways)])  21.2 us
    all_to_all x1, waiting for transfers between devices, local(): lax.all_to_all(outgoing.reshape(device_count, capacity, model_width), ('d...  16.2 us
    dot_general x4, matrix products, key_block(): jnp.einsum('hqk,qhd->khd', grad_scores, split_heads(query_part), preferre...  15.2 us
    dot_general x4, matrix products, key_block(): jnp.einsum('hqk,qhd->khd', weights, split_heads(grad_part), preferred_ele...  13.1 us
    mul x4, local copies, waits for them, and re-layouts, silu_grad(): return sigma * (1.0 + values * (1.0 - sigma))  11.6 us
  transfers between devices with their start and end apart: 8, of which 4 were waited for; matrix products, arithmetic and copies ran while one was open for 25% of the time, Pallas kernels for 0%

profile of v1, /device:TPU:0, one launch (start us, length us, event | category | flops | bytes accessed | tf_op | source)
XLA Modules:
  0.0 388.4 jit_solution(6710774304577252571)
XLA Ops:
  8.0 2.0 scatter_custom_fusion
  10.9 7.3 %all-to-all-start = ((bf16[32,12,512]{2,1,0:T(8,128)(2,1)}), bf16[32,12,512]{2,1,0:T(8,128)(2,1)S(1)}, u32[]{:S(2)}, u32[]{:S(2)}) async-start(bf16[32,12,512]{2,1,0:T(8,128)(2,1)} %reshape.616), calls=%async_computation | async-start | bytes 1048576 | tf_op jit(solution)/shard_map/all_to_all | solution.py:67
  18.4 16.2 %all-to-all-done = bf16[32,12,512]{2,1,0:T(8,128)(2,1)S(1)} async-done(((bf16[32,12,512]{2,1,0:T(8,128)(2,1)}), bf16[32,12,512]{2,1,0:T(8,128)(2,1)S(1)}, u32[]{:S(2)}, u32[]{:S(2)}) %all-to-all-start) | async-done | bytes 393248 | tf_op jit(solution)/shard_map/all_to_all | solution.py:67
  36.2 2.1 multiply_convert_fusion
  41.2 8.1 %collective-permute-done = bf16[256,512]{1,0:T(8,128)(2,1)S(1)} collective-permute-done((bf16[256,512]{1,0:T(8,128)(2,1)}, bf16[256,512]{1,0:T(8,128)(2,1)S(1)}, u32[]{:S(2)}, u32[]{:S(2)}) %collective-permute-start) | collective-permute-done | bytes 262176 | tf_op jit(solution)/shard_map/ppermute | solution.py:14
  56.9 13.0 %collective-permute-done.1 = bf16[512,512]{1,0:T(8,128)(2,1)} collective-permute-done((bf16[512,512]{1,0:T(8,128)(2,1)}, bf16[512,512]{1,0:T(8,128)(2,1)}, u32[]{:S(2)}, u32[]{:S(2)}) %collective-permute-start.1) | collective-permute-done | bytes 524320 | tf_op jit(solution)/shard_map/ppermute | solution.py:14
  70.0 2.9 maximum_select_fusion
  72.9 2.3 copy.48
  75.2 24.0 %while.50 = (s32[]{:T(128)}, f32[256,512]{0,1:T(8,128)S(1)}, bf16[1024,512]{0,1:T(8,128)(2,1)}, s32[256]{0:T(256)S(1)}, s32[4]{0:T(128)S(1)}, /*index=5*/bf16[10...) while((s32[]{:T(128)}, f32[256,512]{0,1:T(8,128)S(1)}, ...), condition=%wide.region_7.8_spmd.clone, body=%wide.region_5.7_spmd.clone.sunk | while | flops 138364160 | bytes 4595917 | solution.py:47
  79.0 2.1 fusion.118
  84.9 2.1 fusion.118
  90.9 2.1 fusion.118
  97.0 2.1 fusion.118
  101.4 2.2 multiply_convert_fusion.1
  104.6 50.2 %while.52 = (s32[]{:T(128)}, f32[256,512]{0,1:T(8,128)}, bf16[1024,512]{1,0:T(8,128)(2,1)}, s32[256]{0:T(256)S(1)}, s32[4]{0:T(128)S(1)}, /*index=5*/bf16[1024,5...) while((s32[]{:T(128)}, f32[256,512]{0,1:T(8,128)}, ...), condition=%wide.region_17.18_spmd.clone, body=%wide.region_15.17_spmd.clone.sunk | while | flops 208094464 | bytes 13508821 | solution.py:47
  106.0 3.3 fusion.133
  109.3 2.9 copy.79
  113.2 2.3 fusion.134
  117.8 3.2 fusion.133
  121.1 2.9 copy.79
  124.9 2.3 fusion.134
  130.6 3.2 fusion.133
  133.8 2.9 copy.79
  137.8 2.3 fusion.134
  143.5 3.2 fusion.133
  146.7 2.9 copy.79
  150.5 2.4 fusion.134
  154.9 2.1 copy.61
  157.0 2.3 fusion.70
  159.3 61.7 %while.51 = (s32[]{:T(128)}, f32[256,512]{0,1:T(8,128)S(1)}, f32[256,512]{0,1:T(8,128)}, bf16[1024,512]{1,0:T(8,128)(2,1)}, s32[4]{0:T(128)S(1)}, /*index=5*/s32...) while((s32[]{:T(128)}, f32[256,512]{0,1:T(8,128)S(1)}, ...), condition=%wide.region_14.15_spmd.clone, body=%wide.region_12.14_spmd.clone.sunk | while | flops 279135488 | bytes 18555156 | solution.py:47
  160.4 2.8 fusion.125
  165.3 3.8 fusion.127
  169.1 3.3 fusion.126
  175.9 2.8 fusion.125
  180.7 3.8 fusion.127
  184.5 3.3 fusion.126
  191.3 2.8 fusion.125
  196.1 3.8 fusion.127
  199.9 3.3 fusion.126
  206.7 2.8 fusion.125
  211.5 3.8 fusion.127
  215.4 3.3 fusion.126
  221.0 2.0 copy.60
  224.0 3.0 fusion.45
  227.0 2.9 fusion.63
  229.9 2.1 fusion.46
  234.0 141.8 %all-reduce.3.cloned.1.call-done = (f32[512,2048]{1,0:T(8,128)}, f32[512,512]{1,0:T(8,128)}) async-done(((f32[512,2048]{1,0:T(8,128)}, f32[512,512]{1,0:T(8,128)}), (f32[512,2048]{1,0:T(8,128)}, f32[512,512]{1,0:T(8,128)})) %all-reduce.3.cloned.1.call-update) | async-done | bytes 5242896 | tf_op jit(solution)/shard_map/psum | solution.py:223
  375.7 5.0 %broadcast_multiply_fusion = f32[512,2048]{1,0:T(8,128)} fusion(f32[512,2048]{1,0:T(8,128)} %get-tuple-element.919), kind=kLoop, calls=%fused_computation.106 | loop fusion | flops 1048576 | bytes 8388608 | tf_op jit(solution)/shard_map/mul | solution.py:225
  (180 shorter events, 74.8 us)
Async XLA Ops:
  7.2 29.0 %copy-start = (bf16[512,2048]{1,0:T(8,128)(2,1)S(1)}, bf16[512,2048]{1,0:T(8,128)(2,1)}, u32[]{:S(2)}) copy-start(bf16[512,2048]{1,0:T(8,128)(2,1)} %param.17) | copy-start | bytes 6291460
  7.2 11.1 %copy-start.10 = (s32[256]{0:T(256)S(1)}, s32[256]{0:T(256)}, u32[]{:S(2)}) copy-start(s32[256]{0:T(256)} %param.15) | copy-start | bytes 3076
  10.9 23.6 %all-to-all-start = ((bf16[32,12,512]{2,1,0:T(8,128)(2,1)}), bf16[32,12,512]{2,1,0:T(8,128)(2,1)S(1)}, u32[]{:S(2)}, u32[]{:S(2)}) async-start(bf16[32,12,512]{2,1,0:T(8,128)(2,1)} %reshape.616), calls=%async_computation | async-start | bytes 1048576 | tf_op jit(solution)/shard_map/all_to_all | solution.py:67
  18.3 54.6 %all-gather.5.cloned.1.call-start = ((), (), s32[]{:S(2)}) async-start(), calls=%async_computation.1 | async-start | bytes 1310720 | tf_op jit(solution)/shard_map/all_gather | solution.py:143
  38.3 1.0 copy-start.8
  38.3 14.8 %copy-start.11 = (s32[1,4]{1,0:T(1,128)S(1)}, s32[1,4]{1,0:T(1,128)}, u32[]{:S(2)}) copy-start(s32[1,4]{1,0:T(1,128)} %param.16) | copy-start | bytes 52
  40.1 16.7 %copy-start.5 = (bf16[256,512]{1,0:T(8,128)(2,1)}, bf16[256,512]{1,0:T(8,128)(2,1)S(1)}, u32[]{:S(2)}) copy-start(bf16[256,512]{1,0:T(8,128)(2,1)S(1)} %get-tuple-element.930) | copy-start | bytes 786436
  40.1 15.0 %copy-start.6 = (bf16[256,512]{1,0:T(8,128)(2,1)S(1)}, bf16[256,512]{1,0:T(8,128)(2,1)}, u32[]{:S(2)}) copy-start(bf16[256,512]{1,0:T(8,128)(2,1)} %get-tuple-element.932) | copy-start | bytes 786436
  40.1 64.5 %all-gather.11.cloned.1.call-start = ((), (), s32[]{:S(2)}) async-start(), calls=%async_computation.4 | async-start | bytes 1310720 | tf_op jit(solution)/shard_map/all_gather | solution.py:203
  40.9 118.4 %all-gather.7.cloned.1.call-start = ((), (), s32[]{:S(2)}) async-start(), calls=%async_computation.2 | async-start | bytes 1310720 | tf_op jit(solution)/shard_map/all_gather | solution.py:212
  40.9 8.3 %collective-permute-start = (bf16[256,512]{1,0:T(8,128)(2,1)}, bf16[256,512]{1,0:T(8,128)(2,1)S(1)}, u32[]{:S(2)}, u32[]{:S(2)}) collective-permute-start(bf16[256,512]{1,0:T(8,128)(2,1)} %get-tuple-element.931), channel_id=1, source_target_pairs={{0,1},{1,0},{2,3},{3,2},{4,5},{5,4},{6,7},{7,6},{8,9},{9,8},{10,11... | collective-permute-start | bytes 786440 | tf_op jit(solution)/shard_map/ppermute | solution.py:14
  51.2 18.7 %collective-permute-start.1 = (bf16[512,512]{1,0:T(8,128)(2,1)}, bf16[512,512]{1,0:T(8,128)(2,1)}, u32[]{:S(2)}, u32[]{:S(2)}) collective-permute-start(bf16[512,512]{1,0:T(8,128)(2,1)} %maximum_select_fusion.1), channel_id=1, source_target_pairs={{0,2},{1,3},{2,0},{3,1},{4,6},{5,7},{6,4},{7,5},{8,10},{9,11},{10,... | collective-permute-start | bytes 1572872 | tf_op jit(solution)/shard_map/ppermute | solution.py:14
  56.9 102.4 %all-gather.9.cloned.1.call-start = ((), (), s32[]{:S(2)}) async-start(), calls=%async_computation.3 | async-start | bytes 1310720 | tf_op jit(solution)/shard_map/all_gather | solution.py:213
  103.5 0.8 copy-start.4
  104.4 271.3 %all-reduce.3.cloned.1.call-start = ((), (), s32[]{:S(2)}) async-start(), calls=%async_computation.5 | async-start | bytes 10485760 | tf_op jit(solution)/shard_map/psum | solution.py:223
  154.9 4.4 %copy-start.1 = (f32[256,512]{0,1:T(8,128)S(1)}, f32[256,512]{0,1:T(8,128)}, u32[]{:S(2)}) copy-start(f32[256,512]{0,1:T(8,128)} %custom-call.1) | copy-start | bytes 1572868
  169.1 3.3 copy-start.2
  173.9 0.8 copy-start.3
  184.5 3.3 copy-start.2
  189.3 0.8 copy-start.3
  199.9 3.3 copy-start.2
  204.8 0.8 copy-start.3
  215.3 3.3 copy-start.2
  220.2 0.8 copy-start.3
  232.0 1.0 copy-start.7
  375.7 5.0 %copy-start.9 = (f32[512,512]{1,0:T(8,128)S(1)}, f32[512,512]{1,0:T(8,128)}, u32[]{:S(2)}) copy-start(f32[512,512]{1,0:T(8,128)} %get-tuple-element.920) | copy-start | bytes 3145732
Sparse Core Ops, SparseCore 0:
  40.3 29.4 all-gather.4
  72.2 25.1 all-gather.10
  99.2 26.5 all-gather.6
  127.5 26.4 all-gather.8
  230.0 145.6 all-reduce.2
